TPU v7x, 512 devices: a whole 4x8x8 slice. The times are simulated.
512 devices in a mesh: dom: 8 (over y_hi, core), fsdp: 64 (over x, z, y_lo).
Axes of the slice: x: 4, y: 8 (y_hi: 4, y_lo: 2; y = y_hi * 2 + y_lo), z: 8, core: 2. Of those that a mesh axis runs over, the one named last changes fastest.
Arguments:
- weights: bfloat16 [8, 64, 640, 896], P('dom', 'fsdp'), may hold values from -6 to 6
- activations: bfloat16 [8, 2, 1280, 2560], P('dom', None, 'fsdp'), may hold values from -6 to 6
- cotangents: bfloat16 [8, 2, 1280, 14336], P('dom', None, 'fsdp'), may hold values from -0.15625 to 0.15625
- lengths: int32 [8, 2, 64], P('dom', None, 'fsdp'), may hold values from 1 to 20, 960 in all within a row
Outputs:
- merged: bfloat16 [64, 640, 896], P('fsdp')
Inputs may be any that keep to these rules, and one draw needn't show every extreme that they name: In every domain and micro-batch the lengths sum to 960, and some block is full.
All inputs are finite; a program needn't handle non-finite values.
Results may differ from a plain program's by a relative error of at most 0.018.
Values may be sent and summed in bfloat16 or wider, within the bound.
No kernel may reach another device: no remote copies, remote signals or barrier semaphores. Data moves between devices by JAX's collectives and lax.ppermute only.
A program may use at most 64 MiB of HBM per device.

v0:
```python
import jax
import jax.numpy as jnp
from jax import lax
from jax.sharding import PartitionSpec as P

damping = 0.001


def squares(pieces):
    feat_rows, cot_rows = pieces
    grad = jnp.einsum("nmsr,nmsc->mrc", feat_rows, cot_rows, preferred_element_type=jnp.float32)
    return grad * grad


def body(weights, activations, cotangents, lengths):
    devices = lax.axis_size("fsdp")
    rows = weights.shape[2]
    cols = weights.shape[3]
    batches = activations.shape[1]
    slots = activations.shape[2]
    row_blocks = activations.shape[3] // rows
    col_blocks = devices // row_blocks
    mask = (jnp.arange(slots)[None, :] < lengths[0, :, 0:1]).astype(jnp.bfloat16)
    feats = activations[0] * mask[:, :, None]
    feat_blocks = feats.reshape(batches, slots, row_blocks, rows).transpose(2, 0, 1, 3)
    feat_send = jnp.broadcast_to(
        feat_blocks[:, None], (row_blocks, col_blocks, batches, slots, rows)
    ).reshape(devices, batches, slots, rows)
    cot_blocks = cotangents[0].reshape(batches, slots, col_blocks, cols).transpose(2, 0, 1, 3)
    cot_send = jnp.broadcast_to(
        cot_blocks[None], (row_blocks, col_blocks, batches, slots, cols)
    ).reshape(devices, batches, slots, cols)
    squared = squares(
        (
            lax.all_to_all(feat_send, "fsdp", split_axis=0, concat_axis=0, tiled=True),
            lax.all_to_all(cot_send, "fsdp", split_axis=0, concat_axis=0, tiled=True),
        )
    )
    fisher = jnp.sum(squared, axis=0) / batches
    term = fisher + damping
    numer_term = term * weights[0, 0].astype(jnp.float32)
    numer, denom = (
        lax.psum(numer_term.astype(jnp.bfloat16), "dom").astype(jnp.float32),
        lax.psum(term.astype(jnp.bfloat16), "dom").astype(jnp.float32),
    )
    merged = (numer / denom).astype(jnp.bfloat16)
    return merged[None]


def solution(mesh):
    return jax.shard_map(
        body,
        mesh=mesh,
        in_specs=(
            P("dom", "fsdp", None, None),
            P("dom", None, "fsdp", None),
            P("dom", None, "fsdp", None),
            P("dom", None, "fsdp"),
        ),
        out_specs=P("fsdp", None, None),
        check_vma=False,
    )
```

profile of v0, /device:TPU:19, one launch (start us, length us, event | category | flops | bytes accessed | tf_op | source)
XLA Modules:
  0.0 328.0 jit_solution(18246231903309940472)
XLA Ops:
  6.5 1.1 squeeze.2
  7.6 0.7 fusion.11
  8.3 0.2 multiply_bitcast_fusion
  8.4 0.2 copy.11
  8.6 3.4 %broadcast_in_dim.6 = bf16[4,16,2,20,640]{4,2,3,1,0:T(2,128)(2,1)} broadcast(bf16[4,2,20,640]{3,1,2,0:T(2,128)(2,1)S(1)} %copy.11), dimensions={0,2,3,4} | broadcast | bytes 3481600 | tf_op jit(solution)/shard_map/broadcast_in_dim | solution.py:26
  12.0 0.0 copy-start
  12.0 14.6 %all-to-all-start = ((bf16[64,2,20,640]{3,1,2,0:T(2,128)(2,1)}), bf16[64,2,20,640]{3,1,2,0:T(2,128)(2,1)}, u32[]{:S(2)}, u32[]{:S(2)}) async-start(bf16[64,2,20,640]{3,1,2,0:T(2,128)(2,1)} %bitcast.2), calls=%async_computation | async-start | bytes 6553600 | tf_op jit(solution)/shard_map/all_to_all | solution.py:35
  26.6 0.0 all-reduce.3.cloned.1.call-start
  26.6 0.0 copy-done
  26.7 0.8 reshape_squeeze.3
  27.4 0.9 copy.12
  28.3 70.1 %all-to-all-done = bf16[64,2,20,640]{3,1,2,0:T(2,128)(2,1)} async-done(((bf16[64,2,20,640]{3,1,2,0:T(2,128)(2,1)}), bf16[64,2,20,640]{3,1,2,0:T(2,128)(2,1)}, u32[]{:S(2)}, u32[]{:S(2)}) %all-to-all-start) | async-done | bytes 3276832 | tf_op jit(solution)/shard_map/all_to_all | solution.py:35
  98.4 4.4 %broadcast_in_dim.7 = bf16[4,16,2,20,896]{4,2,3,1,0:T(2,128)(2,1)} broadcast(bf16[16,2,20,896]{3,1,2,0:T(2,128)(2,1)S(1)} %copy.12), dimensions={1,2,3,4} | broadcast | bytes 5734400 | tf_op jit(solution)/shard_map/broadcast_in_dim | solution.py:30
  102.8 114.7 %all_to_all.10 = bf16[64,2,20,896]{3,1,2,0:T(2,128)(2,1)S(1)} all-to-all(bf16[64,2,20,896]{3,1,2,0:T(2,128)(2,1)} %bitcast.20), channel_id=1, replica_groups=mesh['dom'=8,'fsdp'=64] {'fsdp'}, dimensions={0} | all-to-all | bytes 9175040 | tf_op jit(solution)/shard_map/all_to_all | solution.py:36
  217.5 0.0 copy-start.1
  217.5 5.8 %fusion = f32[640,896]{1,0:T(8,128)S(1)} fusion(bf16[64,2,20,896]{3,1,2,0:T(2,128)(2,1)S(1)} %all_to_all.10, bf16[64,2,20,640]{3,1,2,0:T(2,128)(2,1)} %all-to-all-done), kind=kOutput, calls=%fused_computation.1 | convolution fusion | flops 2937733120 | bytes 10158080 | tf_op jit(solution)/shard_map/nmsr,nmsc->mrc/dot_general | solution.py:11
  223.4 0.0 copy-done.1
  223.4 1.8 fusion.4
  225.1 0.0 all-reduce.3.cloned.1.call-update
  225.2 93.0 %all-reduce.3.cloned.1.call-done = (bf16[640,896]{1,0:T(8,128)(2,1)}, bf16[640,896]{1,0:T(8,128)(2,1)}) async-done(((bf16[640,896]{1,0:T(8,128)(2,1)}, bf16[640,896]{1,0:T(8,128)(2,1)}), (bf16[640,896]{1,0:T(8,128)(2,1)}, bf16[640,896]{1,0:T(8,128)(2,1)})) %all-reduce.3.cloned.1.call-update) | async-done | bytes 2293776 | tf_op jit(solution)/shard_map/psum | solution.py:44
  318.2 3.0 fusion.10
Async XLA Ops:
  12.0 14.7 %copy-start = (bf16[1,2,20,14336]{3,1,2,0:T(2,128)(2,1)S(1)}, bf16[1,2,20,14336]{3,1,2,0:T(2,128)(2,1)}, u32[]{:S(2)}) copy-start(bf16[1,2,20,14336]{3,1,2,0:T(2,128)(2,1)} %param.6) | copy-start | bytes 3440644
  12.0 86.5 %all-to-all-start = ((bf16[64,2,20,640]{3,1,2,0:T(2,128)(2,1)}), bf16[64,2,20,640]{3,1,2,0:T(2,128)(2,1)}, u32[]{:S(2)}, u32[]{:S(2)}) async-start(bf16[64,2,20,640]{3,1,2,0:T(2,128)(2,1)} %bitcast.2), calls=%async_computation | async-start | bytes 6553600 | tf_op jit(solution)/shard_map/all_to_all | solution.py:35
  26.6 291.6 %all-reduce.3.cloned.1.call-start = ((), (), s32[]{:S(2)}) async-start(), calls=%async_computation.2 | async-start | bytes 4587520 | tf_op jit(solution)/shard_map/psum | solution.py:44
  217.5 5.8 %copy-start.1 = (bf16[1,1,640,896]{3,2,1,0:T(8,128)(2,1)S(1)}, bf16[1,1,640,896]{3,2,1,0:T(8,128)(2,1)}, u32[]{:S(2)}) copy-start(bf16[1,1,640,896]{3,2,1,0:T(8,128)(2,1)} %param.4) | copy-start | bytes 3440644
Sparse Core Ops, SparseCore 0:
  225.3 92.8 all-reduce.2
where the time goes:
time: 328 us
  waiting for transfers between devices  163 us (50%)
  blocking collectives  115 us (35%)
  starting transfers between devices  14.7 us (4%)
  between operations  13.5 us (4%)
  local copies, waits for them, and re-layouts  10.7 us (3%)
  matrix products  5.84 us (2%)
  other arithmetic  5.63 us (2%)
    all_to_all x1, blocking collectives, body(): lax.all_to_all(cot_send, 'fsdp', split_axis=0, concat_axis=0, tiled=True)  115 us
    psum x1, waiting for transfers between devices, body(): lax.psum(term.astype(jnp.bfloat16), 'dom').astype(jnp.float32)  93 us
    all_to_all x1, waiting for transfers between devices, body(): lax.all_to_all(feat_send, 'fsdp', split_axis=0, concat_axis=0, tiled=True)  70.1 us
    all_to_all x1, starting transfers between devices, body(): lax.all_to_all(feat_send, 'fsdp', split_axis=0, concat_axis=0, tiled=True)  14.6 us
  transfers between devices with their start and end apart: 2, of which 2 were waited for; matrix products, arithmetic and copies ran while one was open for 1% of the time, Pallas kernels for 0%

commit v1 on v0

--- a/solution.py
+++ b/solution.py
@@ -39,9 +39,12 @@
     fisher = jnp.sum(squared, axis=0) / batches
     term = fisher + damping
     numer_term = term * weights[0, 0].astype(jnp.float32)
+    load_pieces_all = lambda local_block, axis_tag: lax.all_gather(local_block, axis_tag).sum(
+        axis=0
+    )
     numer, denom = (
         lax.psum(numer_term.astype(jnp.bfloat16), "dom").astype(jnp.float32),
-        lax.psum(term.astype(jnp.bfloat16), "dom").astype(jnp.float32),
+        load_pieces_all(term.astype(jnp.bfloat16), "dom").astype(jnp.float32),
     )
     merged = (numer / denom).astype(jnp.bfloat16)
     return merged[None]

time: 328 us -> 417 us (1.27)
  the two profiles are of different devices: /device:TPU:19 before, /device:TPU:17 now
where the time goes in v1:
time: 417 us; the launch traced here: 416 us
  waiting for transfers between devices  248 us (59%)
  blocking collectives  112 us (27%)
  starting transfers between devices  15 us (4%)
  between operations  13.5 us (3%)
  other arithmetic  10.9 us (3%)
  local copies, waits for them, and re-layouts  10.7 us (3%)
  matrix products  5.84 us (1%)
    all_to_all x1, blocking collectives, body(): lax.all_to_all(cot_send, 'fsdp', split_axis=0, concat_axis=0, tiled=True)  112 us
    all_gather x1, waiting for transfers between devices, body(): lax.all_gather(local_block, axis_tag).sum(axis=0)  94.9 us
    psum x1, waiting for transfers between devices, body(): lax.psum(numer_term.astype(jnp.bfloat16), 'dom').astype(jnp.float32)  80.4 us
    all_to_all x1, waiting for transfers between devices, body(): lax.all_to_all(feat_send, 'fsdp', split_axis=0, concat_axis=0, tiled=True)  72.4 us
    all_to_all x1, starting transfers between devices, body(): lax.all_to_all(feat_send, 'fsdp', split_axis=0, concat_axis=0, tiled=True)  14.9 us
  transfers between devices with their start and end apart: 3, of which 3 were waited for; matrix products, arithmetic and copies ran while one was open for 2% of the time, Pallas kernels for 0%

profile of v1, /device:TPU:17, one launch (start us, length us, event | category | flops | bytes accessed | tf_op | source)
XLA Modules:
  0.0 416.3 jit_solution(13682991294371484641)
XLA Ops:
  6.5 1.1 squeeze.2
  7.6 0.7 fusion.11
  8.3 0.2 multiply_bitcast_fusion
  8.4 0.2 copy.11
  8.6 3.4 broadcast_in_dim.6
  12.0 0.0 copy-start
  12.0 14.9 %all-to-all-start = ((bf16[64,2,20,640]{3,1,2,0:T(2,128)(2,1)}), bf16[64,2,20,640]{3,1,2,0:T(2,128)(2,1)}, u32[]{:S(2)}, u32[]{:S(2)}) async-start(bf16[64,2,20,640]{3,1,2,0:T(2,128)(2,1)} %bitcast.2), calls=%async_computation | async-start | bytes 6553600 | tf_op jit(solution)/shard_map/all_to_all | solution.py:35
  26.9 0.0 all-gather.3.cloned.1.call-start
  26.9 0.0 copy-done
  26.9 0.8 reshape_squeeze.3
  27.7 0.9 copy.12
  28.6 72.4 %all-to-all-done = bf16[64,2,20,640]{3,1,2,0:T(2,128)(2,1)} async-done(((bf16[64,2,20,640]{3,1,2,0:T(2,128)(2,1)}), bf16[64,2,20,640]{3,1,2,0:T(2,128)(2,1)}, u32[]{:S(2)}, u32[]{:S(2)}) %all-to-all-start) | async-done | bytes 3276832 | tf_op jit(solution)/shard_map/all_to_all | solution.py:35
  101.0 4.4 %broadcast_in_dim.7 = bf16[4,16,2,20,896]{4,2,3,1,0:T(2,128)(2,1)} broadcast(bf16[16,2,20,896]{3,1,2,0:T(2,128)(2,1)S(1)} %copy.12), dimensions={1,2,3,4} | broadcast | bytes 5734400 | tf_op jit(solution)/shard_map/broadcast_in_dim | solution.py:30
  105.4 112.1 %all_to_all.10 = bf16[64,2,20,896]{3,1,2,0:T(2,128)(2,1)S(1)} all-to-all(bf16[64,2,20,896]{3,1,2,0:T(2,128)(2,1)} %bitcast.21), channel_id=1, replica_groups=mesh['dom'=8,'fsdp'=64] {'fsdp'}, dimensions={0} | all-to-all | bytes 9175040 | tf_op jit(solution)/shard_map/all_to_all | solution.py:36
  217.5 5.8 %fusion = f32[640,896]{1,0:T(8,128)S(1)} fusion(bf16[64,2,20,896]{3,1,2,0:T(2,128)(2,1)S(1)} %all_to_all.10, bf16[64,2,20,640]{3,1,2,0:T(2,128)(2,1)} %all-to-all-done), kind=kOutput, calls=%fused_computation.1 | convolution fusion | flops 2937733120 | bytes 10158080 | tf_op jit(solution)/shard_map/nmsr,nmsc->mrc/dot_general | solution.py:11
  223.3 0.0 copy-done.1
  223.4 1.8 fusion.4
  225.1 0.0 all-gather.3.cloned.1.call-update
  225.2 0.0 all-reduce.2.cloned.1.call-start
  225.2 0.7 all-reduce.2.cloned.1.call-update
  225.9 94.9 %all-gather.3.cloned.1.call-done = bf16[5120,896]{1,0:T(8,128)(2,1)} async-done(((bf16[640,896]{1,0:T(8,128)(2,1)}), bf16[5120,896]{1,0:T(8,128)(2,1)}) %all-gather.3.cloned.1.call-update) | async-done | bytes 9175056 | tf_op jit(solution)/shard_map/all_gather | solution.py:42
  320.8 5.6 %reduce_sum.22 = bf16[640,896]{1,0:T(8,128)(2,1)S(1)} reduce(bf16[8,640,896]{2,1,0:T(8,128)(2,1)} %bitcast.22, bf16[]{:T(256)} %constant.8.clone.1), dimensions={0}, to_apply=%region_2.0 | reduce | flops 4014080 | bytes 10321922 | tf_op jit(solution)/shard_map/reduce_sum | solution.py:42
  326.4 80.4 %all-reduce.2.cloned.1.call-done = bf16[640,896]{1,0:T(8,128)(2,1)} async-done(((bf16[640,896]{1,0:T(8,128)(2,1)}), bf16[640,896]{1,0:T(8,128)(2,1)}) %all-reduce.2.cloned.1.call-update) | async-done | bytes 1146896 | tf_op jit(solution)/shard_map/psum | solution.py:46
  406.8 2.7 fusion.10
  (1 shorter events, 0.0 us)
Async XLA Ops:
  12.0 14.9 %copy-start = (bf16[1,2,20,14336]{3,1,2,0:T(2,128)(2,1)S(1)}, bf16[1,2,20,14336]{3,1,2,0:T(2,128)(2,1)}, u32[]{:S(2)}) copy-start(bf16[1,2,20,14336]{3,1,2,0:T(2,128)(2,1)} %param.6) | copy-start | bytes 3440644
  12.0 89.0 %all-to-all-start = ((bf16[64,2,20,640]{3,1,2,0:T(2,128)(2,1)}), bf16[64,2,20,640]{3,1,2,0:T(2,128)(2,1)}, u32[]{:S(2)}, u32[]{:S(2)}) async-start(bf16[64,2,20,640]{3,1,2,0:T(2,128)(2,1)} %bitcast.2), calls=%async_computation | async-start | bytes 6553600 | tf_op jit(solution)/shard_map/all_to_all | solution.py:35
  26.9 293.9 %all-gather.3.cloned.1.call-start = ((), (), s32[]{:S(2)}) async-start(), calls=%async_computation.3 | async-start | bytes 10321920 | tf_op jit(solution)/shard_map/all_gather | solution.py:42
  217.5 5.9 %copy-start.1 = (bf16[1,1,640,896]{3,2,1,0:T(8,128)(2,1)S(1)}, bf16[1,1,640,896]{3,2,1,0:T(8,128)(2,1)}, u32[]{:S(2)}) copy-start(bf16[1,1,640,896]{3,2,1,0:T(8,128)(2,1)} %param.4) | copy-start | bytes 3440644
  225.2 181.6 %all-reduce.2.cloned.1.call-start = ((), (), s32[]{:S(2)}) async-start(), calls=%async_computation.2 | async-start | bytes 2293760 | tf_op jit(solution)/shard_map/psum | solution.py:46
Sparse Core Ops, SparseCore 0:
  225.3 95.4 all-gather.2
  323.7 83.0 all-reduce.1
